TPU v7x, 256 devices: a whole 4x4x8 slice. The times are simulated.
256 devices in a mesh: dp: 32 (over z, y), row: 2 (over core), col: 4 (over x).
Axes of the slice: x: 4, y: 4, z: 8, core: 2. Of those that a mesh axis runs over, the one named last changes fastest.
Arguments:
- x_input: bfloat16 [32, 32, 64, 640], P('dp', 'row', 'col'), may hold values from -6 to 6
- pre_act: bfloat16 [32, 32, 64, 640], P('dp', 'row', 'col'), may hold values from -6 to 6
- out_grad: bfloat16 [32, 32, 64, 640], P('dp', 'row', 'col'), may hold values from -0.15625 to 0.15625
- conv_weight: bfloat16 [3, 3, 640, 640], replicated, may hold values from -0.078125 to 0.078125
- q_prev: float32 [5760, 2, 64], replicated, may hold values from -6 to 6
Outputs:
- p_basis: float32 [640, 2, 64], P('dp')
- q_next: float32 [5760, 2, 64], P('dp')
All inputs are finite; a program needn't handle non-finite values.
Results may differ from a plain program's by a relative error of at most 0.0036.
Values may be sent and summed in bfloat16 or wider, within the bound.
A program may use at most 128 MiB of HBM per device.

v0:
```python
import jax
import jax.numpy as jnp
from jax import lax
from jax.sharding import PartitionSpec as P


def padded_2(value, sides, width):
    for axis, dim in sides:
        size, length = (lax.axis_size(axis), value.shape[dim])
        up = [(i, (i + 1) % size) for i in range(size - 1)]
        down = [(j, i) for i, j in up]
        last = lax.slice_in_dim(value, length - width, length, axis=dim)
        leading = lax.slice_in_dim(value, 0, width, axis=dim)
        before = lax.ppermute(last, axis, up)
        after = lax.ppermute(leading, axis, down)
        value = jnp.concatenate([before, value, after], axis=dim)
    return value


def silu_slope(pre_float):
    sigma = jax.nn.sigmoid(pre_float)
    return sigma * (1.0 + pre_float * (1.0 - sigma))


def contract_first(left, right, exact):
    if exact:
        return lax.dot_general(
            left,
            right,
            (((0,), (0,)), ((), ())),
            precision=lax.Precision.HIGHEST,
            preferred_element_type=jnp.float32,
        )
    return lax.dot_general(
        left, right, (((0,), (0,)), ((), ())), preferred_element_type=jnp.float32
    )


def tap_window(padded, shift_row, shift_col, height, breadth):
    return padded[
        1 + shift_row : 1 + shift_row + height, 1 + shift_col : 1 + shift_col + breadth, :
    ].reshape(height * breadth, padded.shape[2])


def column_terms(moments, q_prev):
    return jnp.stack(
        [contract_first(moments[layer], q_prev[:, layer, :], True) for layer in range(2)], axis=1
    )


def row_terms(moments, ortho_basis):
    return jnp.stack(
        [
            jnp.dot(
                moments[layer],
                ortho_basis[:, layer, :],
                precision=lax.Precision.HIGHEST,
                preferred_element_type=jnp.float32,
            )
            for layer in range(2)
        ],
        axis=1,
    )


def gram_of(power_raw):
    return jnp.einsum(
        "mqn,mqg->qng",
        power_raw,
        power_raw,
        precision=lax.Precision.HIGHEST,
        preferred_element_type=jnp.float32,
    )


def orthonormal(power_raw, gram_matrix):
    bases = []
    for layer in range(2):
        lower = jnp.linalg.cholesky(gram_matrix[layer])
        bases.append(
            lax.linalg.triangular_solve(
                lower, power_raw[:, layer, :], left_side=False, lower=True, transpose_a=True
            )
        )
    return jnp.stack(bases, axis=1)


def on_device(x_input, pre_act, out_grad, conv_weight, q_prev):
    height, breadth, channels = (x_input.shape[1], x_input.shape[2], x_input.shape[3])
    pixels = height * breadth
    input_tile = x_input.reshape(height, breadth, channels)
    grad_tile = out_grad.reshape(height, breadth, channels)
    pre_float = pre_act.reshape(pixels, channels).astype(jnp.float32)
    hidden_flat = jax.nn.silu(pre_float).astype(jnp.bfloat16)
    grad_pad = padded_2(grad_tile, (("row", 0), ("col", 1)), 1)
    back_grad = jnp.zeros((pixels, channels), jnp.float32)
    second_taps = []
    for shift_row in (-1, 0, 1):
        for shift_col in (-1, 0, 1):
            window = tap_window(grad_pad, -shift_row, -shift_col, height, breadth)
            back_grad = back_grad + lax.dot_general(
                window,
                conv_weight[shift_row + 1, shift_col + 1],
                (((1,), (1,)), ((), ())),
                preferred_element_type=jnp.float32,
            )
            second_taps.append(contract_first(hidden_flat, window, False))
    pre_grad = (back_grad * silu_slope(pre_float)).astype(jnp.bfloat16)
    first_taps = []
    deriv_pad = padded_2(pre_grad.reshape(height, breadth, channels), (("row", 0), ("col", 1)), 1)
    input_flat = input_tile.reshape(pixels, channels)
    for shift_row in (-1, 0, 1):
        for shift_col in (-1, 0, 1):
            first_taps.append(
                contract_first(
                    input_flat,
                    tap_window(deriv_pad, -shift_row, -shift_col, height, breadth),
                    False,
                )
            )
    moments = jnp.stack(
        [
            jnp.stack(first_taps).reshape(9 * channels, channels),
            jnp.stack(second_taps).reshape(9 * channels, channels),
        ]
    )
    kernel_rows = moments.shape[1]
    owner = lax.axis_index("dp")
    basis_count = channels // lax.axis_size("dp")
    factor_count = kernel_rows // lax.axis_size("dp")
    power_raw = column_terms(moments, q_prev)
    for axis in ("row", "col", "dp"):
        power_raw = lax.psum(power_raw, axis)
    ortho_basis = orthonormal(power_raw, gram_of(power_raw))
    factor_out = lax.psum_scatter(
        row_terms(moments, ortho_basis), "dp", scatter_dimension=0, tiled=True
    )
    for axis in ("row", "col"):
        factor_out = lax.psum(factor_out, axis)
    basis_out = lax.dynamic_slice_in_dim(ortho_basis, owner * basis_count, basis_count, 0)
    return (basis_out, factor_out)


def solution(mesh):
    placed = (
        P("dp", "row", "col", None),
        P("dp", "row", "col", None),
        P("dp", "row", "col", None),
        P(),
        P(),
    )
    return jax.shard_map(
        on_device,
        mesh=mesh,
        in_specs=placed,
        out_specs=(P("dp", None, None), P("dp", None, None)),
        check_vma=False,
    )
```

profile of v0, /device:TPU:8, one launch (start us, length us, event | category | flops | bytes accessed | tf_op | source)
XLA Modules:
  0.0 609.8 jit_solution(7711296566547497687)
XLA Ops:
  7.2 0.8 slice_bitcast_fusion.9
  8.0 1.3 collective-permute-start.1
  9.3 3.0 collective-permute-start
  12.3 1.2 fusion.43
  13.5 1.2 fusion.38
  14.7 1.1 pad_maximum_fusion.11
  15.8 3.4 collective-permute-start.3
  19.2 1.3 collective-permute-start.2
  20.5 1.1 pad_maximum_fusion.5
  21.7 1.6 fusion.23
  23.3 1.9 collective-permute-done.2
  25.2 1.3 maximum_maximum_fusion
  26.7 0.5 bitcast_dynamic-update-slice_fusion.17
  27.1 0.5 bitcast_dynamic-update-slice_fusion.16
  27.6 0.5 bitcast_dynamic-update-slice_fusion.15
  28.1 0.5 bitcast_dynamic-update-slice_fusion.14
  28.6 0.5 bitcast_dynamic-update-slice_fusion.13
  29.1 1.1 slice-done.4
  30.3 1.1 slice-done.5
  31.8 0.5 bitcast_dynamic-update-slice_fusion.12
  32.3 0.5 bitcast_dynamic-update-slice_fusion.11
  32.8 0.5 bitcast_dynamic-update-slice_fusion.10
  33.3 0.5 bitcast_dynamic-update-slice_fusion.9
  33.7 0.5 convolution_add_fusion.6
  34.2 0.5 convolution_add_fusion.5
  34.7 0.5 convolution_add_fusion.4
  35.2 0.5 convolution_add_fusion.3
  35.6 0.5 convolution_add_fusion.2
  36.1 0.5 convolution_add_fusion.1
  36.6 0.5 fusion.8
  37.1 1.4 collective-permute-start.5
  38.5 3.2 collective-permute-start.4
  41.7 8.8 %fusion.12 = f32[640,1,64]{0,2,1:T(8,128)S(1)} fusion(f32[5760,640]{1,0:T(8,128)S(1)} %bitcast.256, f32[5760,2,64]{0,2,1:T(8,128)S(1)} %copy-done.6), kind=kOutput, calls=%fused_computation.38 | convolution fusion | flops 2831155200 | bytes 16384000 | tf_op jit(solution)/shard_map/dot_general | solution.py:27
  50.7 3.4 collective-permute-start.7
  54.1 1.5 collective-permute-start.6
  55.8 4.2 collective-permute-done.6
  62.4 0.5 bitcast_dynamic-update-slice_fusion.4
  62.9 0.5 bitcast_dynamic-update-slice_fusion.3
  63.3 0.5 bitcast_dynamic-update-slice_fusion.2
  64.7 9.3 %fusion.9 = f32[640,1,64]{0,2,1:T(8,128)S(1)} fusion(f32[5760,640]{1,0:T(8,128)S(1)} %bitcast.252, f32[5760,2,64]{0,2,1:T(8,128)S(1)} %copy-done.6), kind=kOutput, calls=%fused_computation.37 | convolution fusion | flops 2831155200 | bytes 16384000 | tf_op jit(solution)/shard_map/dot_general | solution.py:27
  74.0 0.7 pad_maximum_fusion.7
  74.8 31.2 %all-reduce.8.cloned.1.call-done = f32[640,2,64]{0,2,1:T(8,128)} async-done(((f32[640,2,64]{0,2,1:T(8,128)}), f32[640,2,64]{0,2,1:T(8,128)}) %all-reduce.8.cloned.1.call-update) | async-done | bytes 327696 | tf_op jit(solution)/shard_map/psum | solution.py:133
  106.1 50.8 %all-reduce.10.cloned.1.call-done = f32[640,2,64]{0,2,1:T(8,128)} async-done(((f32[640,2,64]{0,2,1:T(8,128)}), f32[640,2,64]{0,2,1:T(8,128)}) %all-reduce.10.cloned.1.call-update) | async-done | bytes 327696 | tf_op jit(solution)/shard_map/psum | solution.py:133
  156.9 148.6 %all-reduce.12.cloned.1.call-done = f32[640,2,64]{0,2,1:T(8,128)} async-done(((f32[640,2,64]{0,2,1:T(8,128)}), f32[640,2,64]{0,2,1:T(8,128)}) %all-reduce.12.cloned.1.call-update) | async-done | bytes 327696 | tf_op jit(solution)/shard_map/psum | solution.py:133
  305.6 1.5 fusion.62
  307.3 5.8 cholesky.44
  313.2 0.6 compare_reduce_fusion.1
  313.8 0.7 fusion.50
  314.5 4.9 custom-call.6
  319.4 5.9 cholesky.55
  325.3 0.6 compare_reduce_fusion
  325.9 0.7 fusion.51
  326.6 4.9 custom-call.7
  331.5 1.4 fusion.45
  332.9 17.3 %convolution_bitcast_fusion = f32[5760,1,64]{0,2,1:T(8,128)S(1)} fusion(f32[5760,640]{1,0:T(8,128)} %bitcast.257, f32[64,640]{1,0:T(8,128)S(1)} %fusion.45), kind=kOutput, calls=%fused_computation | convolution fusion | flops 2831155200 | bytes 16384000 | tf_op jit(solution)/shard_map/dot_general | solution.py:54
  350.7 14.2 %convolution_bitcast_fusion.1 = f32[5760,1,64]{0,2,1:T(8,128)S(1)} fusion(f32[5760,640]{1,0:T(8,128)S(1)} %bitcast.255, f32[64,640]{1,0:T(8,128)S(1)} %fusion.46), kind=kOutput, calls=%fused_computation.1 | convolution fusion | flops 2831155200 | bytes 16384000 | tf_op jit(solution)/shard_map/dot_general | solution.py:54
  364.9 1.8 pad_maximum_fusion
  366.8 0.6 dynamic-slice
  368.0 153.1 %all-reduce.18.cloned.1.call-done = f32[5760,2,64]{0,2,1:T(8,128)} async-done(((f32[5760,2,64]{0,2,1:T(8,128)}), f32[5760,2,64]{0,2,1:T(8,128)}) %all-reduce.18.cloned.1.call-update) | async-done | bytes 2949136
  521.1 1.7 constant_dynamic-slice_fusion
  522.9 28.5 %all-reduce.14.cloned.1.call-done = f32[180,2,64]{0,2,1:T(8,128)} async-done(((f32[180,2,64]{0,2,1:T(8,128)}), f32[180,2,64]{0,2,1:T(8,128)}) %all-reduce.14.cloned.1.call-update) | async-done | bytes 92176 | tf_op jit(solution)/shard_map/psum | solution.py:139
  551.4 0.7 copy.16
  552.1 49.0 %all-reduce.16.cloned.1.call-done = f32[180,2,64]{0,2,1:T(8,128)} async-done(((f32[180,2,64]{0,2,1:T(8,128)}), f32[180,2,64]{0,2,1:T(8,128)}) %all-reduce.16.cloned.1.call-update) | async-done | bytes 92176 | tf_op jit(solution)/shard_map/psum | solution.py:139
  601.2 1.6 copy.42
  (70 shorter events, 5.3 us)
Async XLA Ops:
  7.2 53.4 %copy-start = (bf16[1,16,16,640]{3,2,1,0:T(8,128)(2,1)S(1)}, bf16[1,16,16,640]{3,2,1,0:T(8,128)(2,1)}, u32[]{:S(2)}) copy-start(bf16[1,16,16,640]{3,2,1,0:T(8,128)(2,1)} %param.8) | copy-start | bytes 983044
  7.2 98.8 %all-reduce.8.cloned.1.call-start = ((), (), s32[]{:S(2)}) async-start(), calls=%async_computation | async-start | bytes 655360 | tf_op jit(solution)/shard_map/psum | solution.py:133
  8.0 6.7 %collective-permute-start.1 = (bf16[1,16,640]{2,1,0:T(8,128)(2,1)S(1)}, bf16[1,16,640]{2,1,0:T(8,128)(2,1)S(1)}, u32[]{:S(2)}, u32[]{:S(2)}) collective-permute-start(bf16[1,16,640]{2,1,0:T(8,128)(2,1)S(1)} %get-tuple-element.35), channel_id=1, source_target_pairs={{4,0},{5,1},{6,2},{7,3},{12,8},{13,9},{14,10},{15,11},{20,16},{21,... | collective-permute-start | bytes 61448 | tf_op jit(solution)/shard_map/ppermute | solution.py:15
  9.3 5.4 collective-permute-start
  15.8 7.5 %collective-permute-start.3 = (bf16[18,1,640]{2,1,0:T(2,128)(2,1)S(1)}, bf16[18,1,640]{2,1,0:T(2,128)(2,1)S(1)}, u32[]{:S(2)}, u32[]{:S(2)}) collective-permute-start(bf16[18,1,640]{2,1,0:T(2,128)(2,1)S(1)} %get-tuple-element.26), channel_id=1, source_target_pairs={{0,1},{1,2},{2,3},{4,5},{5,6},{6,7},{8,9},{9,10},{10,11},{12,13},{... | collective-permute-start | bytes 69128 | tf_op jit(solution)/shard_map/ppermute | solution.py:14
  19.2 6.0 collective-permute-start.2
  23.3 5.3 copy-start.4
  23.3 5.3 copy-start.7
  28.1 2.2 slice-start.4
  28.6 2.8 slice-start.5
  33.7 8.0 %copy-start.3 = (f32[9,640,640]{2,1,0:T(8,128)}, f32[9,640,640]{2,1,0:T(8,128)S(1)}, u32[]{:S(2)}) copy-start(f32[9,640,640]{2,1,0:T(8,128)S(1)} %bitcast_dynamic-update-slice_fusion.9) | copy-start | bytes 44236804
  34.2 7.5 %copy-start.6 = (f32[5760,2,64]{0,2,1:T(8,128)S(1)}, f32[5760,2,64]{0,2,1:T(8,128)}, u32[]{:S(2)}) copy-start(f32[5760,2,64]{0,2,1:T(8,128)} %param.12) | copy-start | bytes 8847364
  37.1 13.5 %collective-permute-start.5 = (bf16[1,16,640]{2,1,0:T(8,128)(2,1)S(1)}, bf16[1,16,640]{2,1,0:T(8,128)(2,1)S(1)}, u32[]{:S(2)}, u32[]{:S(2)}) collective-permute-start(bf16[1,16,640]{2,1,0:T(8,128)(2,1)S(1)} %get-tuple-element.31), channel_id=1, source_target_pairs={{4,0},{5,1},{6,2},{7,3},{12,8},{13,9},{14,10},{15,11},{20,16},{21,... | collective-permute-start | bytes 61448 | tf_op jit(solution)/shard_map/ppermute | solution.py:15
  38.5 12.1 %collective-permute-start.4 = (bf16[1,16,640]{2,1,0:T(8,128)(2,1)S(1)}, bf16[1,16,640]{2,1,0:T(8,128)(2,1)S(1)}, u32[]{:S(2)}, u32[]{:S(2)}) collective-permute-start(bf16[1,16,640]{2,1,0:T(8,128)(2,1)S(1)} %get-tuple-element.30), channel_id=1, source_target_pairs={{0,4},{1,5},{2,6},{3,7},{8,12},{9,13},{10,14},{11,15},{16,20},{17,... | collective-permute-start | bytes 61448 | tf_op jit(solution)/shard_map/ppermute | solution.py:14
  50.7 5.1 collective-permute-start.7
  54.1 6.0 collective-permute-start.6
  64.7 9.3 %copy-start.2 = (f32[9,640,640]{2,1,0:T(8,128)}, f32[9,640,640]{2,1,0:T(8,128)S(1)}, u32[]{:S(2)}) copy-start(f32[9,640,640]{2,1,0:T(8,128)S(1)} %bitcast_dynamic-update-slice_fusion) | copy-start | bytes 44236804
  74.8 82.1 %all-reduce.10.cloned.1.call-start = ((), (), s32[]{:S(2)}) async-start(), calls=%async_computation.1 | async-start | bytes 655360 | tf_op jit(solution)/shard_map/psum | solution.py:133
  106.0 199.5 %all-reduce.12.cloned.1.call-start = ((), (), s32[]{:S(2)}) async-start(), calls=%async_computation.2 | async-start | bytes 655360 | tf_op jit(solution)/shard_map/psum | solution.py:133
  156.9 364.2 %all-reduce.18.cloned.1.call-start = ((), (), s32[]{:S(2)}) async-start(), calls=%async_computation.5 | async-start | bytes 5898240
  331.5 19.1 %slice-start = ((s8[14745600]{0:T(1024)(128)(4,1)}), s8[4194304]{0:T(1024)(128)(4,1)S(1)}, s32[]{:S(2)}) async-start(s8[14745600]{0:T(1024)(128)(4,1)} %bitcast.253), calls=%async_computation.6 | async-start | bytes 8388608
  332.9 17.3 %copy-start.5 = (f32[640,2,64]{0,2,1:T(8,128)S(1)}, f32[640,2,64]{0,2,1:T(8,128)}, u32[]{:S(2)}) copy-start(f32[640,2,64]{0,2,1:T(8,128)} %all-reduce.12.cloned.1.call-done) | copy-start | bytes 983044
  332.9 17.7 %slice-start.1 = ((s8[14745600]{0:T(1024)(128)(4,1)}), s8[4194304]{0:T(1024)(128)(4,1)S(1)}, s32[]{:S(2)}) async-start(s8[14745600]{0:T(1024)(128)(4,1)} %bitcast.253), calls=%async_computation.7 | async-start | bytes 8388608
  332.9 17.7 %slice-start.2 = ((s8[14745600]{0:T(1024)(128)(4,1)}), s8[4194304]{0:T(1024)(128)(4,1)S(1)}, s32[]{:S(2)}) async-start(s8[14745600]{0:T(1024)(128)(4,1)} %bitcast.253), calls=%async_computation.8 | async-start | bytes 8388608
  332.9 17.7 %slice-start.3 = ((s8[14745600]{0:T(1024)(128)(4,1)}), s8[2162688]{0:T(1024)(128)(4,1)S(1)}, s32[]{:S(2)}) async-start(s8[14745600]{0:T(1024)(128)(4,1)} %bitcast.253), calls=%async_computation.9 | async-start | bytes 4325376
  350.7 252.1 %copy-start.1 = (bf16[1,16,16,640]{3,2,1,0:T(8,128)(2,1)S(1)}, bf16[1,16,16,640]{3,2,1,0:T(8,128)(2,1)}, u32[]{:S(2)}) copy-start(bf16[1,16,16,640]{3,2,1,0:T(8,128)(2,1)} %param.8) | copy-start | bytes 983044
  364.9 1.9 copy-start.8
  366.7 184.6 %all-reduce.14.cloned.1.call-start = ((), (), s32[]{:S(2)}) async-start(), calls=%async_computation.3 | async-start | bytes 262144 | tf_op jit(solution)/shard_map/psum | solution.py:139
  522.8 78.4 %all-reduce.16.cloned.1.call-start = ((), (), s32[]{:S(2)}) async-start(), calls=%async_computation.4 | async-start | bytes 262144 | tf_op jit(solution)/shard_map/psum | solution.py:139
Sparse Core Ops, SparseCore 0:
  74.9 31.0 all-reduce.7
  108.5 48.3 all-reduce.9
  160.7 144.8 all-reduce.11
  366.9 154.2 all-reduce.17
  524.3 27.0 all-reduce.13
  553.6 47.5 all-reduce.15
where the time goes:
time: 616 us; the launch traced here: 610 us
  waiting for transfers between devices  468 us (76%)
  matrix products  66.6 us (11%)
  other arithmetic  33.1 us (5%)
  starting transfers between devices  18.8 us (3%)
  between operations  15.6 us (3%)
  local copies, waits for them, and re-layouts  8.22 us (1%)
    psum x3, waiting for transfers between devices, on_device(): power_raw = lax.psum(power_raw, axis)  231 us
    unnamed x7, waiting for transfers between devices  153 us
    psum x2, waiting for transfers between devices, on_device(): factor_out = lax.psum(factor_out, axis)  77.5 us
    dot_general x2, matrix products, row_terms(): jnp.dot(moments[layer], ortho_basis[:, layer, :], precision=lax.Precision...  31.5 us
    dot_general x2, matrix products, contract_first(): lax.dot_general(left, right, (((0,), (0,)), ((), ())), precision=lax.Prec...  18.1 us
    another operation x6, other arithmetic, orthonormal(): lower = jnp.linalg.cholesky(gram_matrix[layer])  13.1 us
    ppermute x4, starting transfers between devices, padded_2(): before = lax.ppermute(last, axis, up)  13 us
  transfers between devices with their start and end apart: 14, of which 9 were waited for; matrix products, arithmetic and copies ran while one was open for 3% of the time, Pallas kernels for 0%

commit v1 on v0

--- a/solution.py
+++ b/solution.py
@@ -130,7 +130,7 @@
     factor_count = kernel_rows // lax.axis_size("dp")
     power_raw = column_terms(moments, q_prev)
     for axis in ("row", "col", "dp"):
-        power_raw = lax.psum(power_raw, axis)
+        power_raw = jnp.sum(jax.lax.all_gather(power_raw, axis), 0)
     ortho_basis = orthonormal(power_raw, gram_of(power_raw))
     factor_out = lax.psum_scatter(
         row_terms(moments, ortho_basis), "dp", scatter_dimension=0, tiled=True

time: 616 us -> 540 us (0.88)
  waiting for transfers between devices: 468 us -> 373 us
  local copies, waits for them, and re-layouts: 8.22 us -> 17.8 us
  other arithmetic: 33.1 us -> 41.1 us
    psum x3 -> x0, waiting for transfers between devices: 231 us -> none  [on_device(): power_raw = lax.psum(power_raw, axis)]
    all_gather x0 -> x2, waiting for transfers between devices: none -> 140 us  [on_device(): power_raw = jnp.sum(jax.lax.all_gather(power_raw, axis), 0)]
    reduce_sum x0 -> x3, other arithmetic: none -> 8.7 us  [on_device(): power_raw = jnp.sum(jax.lax.all_gather(power_raw, axis), 0)]
    unnamed x34 -> x23, local copies, waits for them, and re-layouts: 6.87 us -> 14.2 us
    unnamed x7 -> x6, waiting for transfers between devices: 153 us -> 153 us
  transfers between devices with their start and end apart: 14 -> 13, of which waited for: 9 -> 7; matrix products, arithmetic and copies ran while one was open for 3% -> 4% of each run, Pallas kernels for 0% -> 0%
where the time goes in v1:
time: 540 us; the launch traced here: 536 us
  waiting for transfers between devices  373 us (69%)
  matrix products  67.2 us (12%)
  other arithmetic  41.1 us (8%)
  starting transfers between devices  19.3 us (4%)
  local copies, waits for them, and re-layouts  17.8 us (3%)
  between operations  15.2 us (3%)
    unnamed x6, waiting for transfers between devices  153 us
    all_gather x2, waiting for transfers between devices, on_device(): power_raw = jnp.sum(jax.lax.all_gather(power_raw, axis), 0)  140 us
    psum x2, waiting for transfers between devices, on_device(): factor_out = lax.psum(factor_out, axis)  77.5 us
    dot_general x2, matrix products, row_terms(): jnp.dot(moments[layer], ortho_basis[:, layer, :], precision=lax.Precision...  34.1 us
    dot_general x2, matrix products, contract_first(): lax.dot_general(left, right, (((0,), (0,)), ((), ())), precision=lax.Prec...  18.1 us
    unnamed x23, local copies, waits for them, and re-layouts  14.2 us
    ppermute x4, starting transfers between devices, padded_2(): before = lax.ppermute(last, axis, up)  13.8 us
    another operation x6, other arithmetic, orthonormal(): lower = jnp.linalg.cholesky(gram_matrix[layer])  13 us
  transfers between devices with their start and end apart: 13, of which 7 were waited for; matrix products, arithmetic and copies ran while one was open for 4% of the time, Pallas kernels for 0%

profile of v1, /device:TPU:8, one launch (start us, length us, event | category | flops | bytes accessed | tf_op | source)
XLA Modules:
  0.0 535.6 jit_solution(1238776194112328869)
XLA Ops:
  7.2 0.9 slice_bitcast_fusion.9
  8.1 2.0 collective-permute-start
  10.1 1.3 collective-permute-start.1
  11.4 1.2 fusion.43
  12.6 1.2 fusion.38
  13.8 1.1 pad_maximum_fusion.11
  14.9 1.3 collective-permute-start.2
  16.2 4.5 collective-permute-start.3
  20.8 1.1 pad_maximum_fusion.5
  21.9 1.6 fusion.23
  23.6 1.3 maximum_maximum_fusion
  25.6 0.5 convolution_add_fusion.6
  26.0 0.5 convolution_add_fusion.5
  26.5 0.5 convolution_add_fusion.4
  27.0 0.5 convolution_add_fusion.3
  27.5 0.5 convolution_add_fusion.2
  28.0 0.5 convolution_add_fusion.1
  28.4 0.5 fusion.8
  28.9 2.5 collective-permute-start.4
  31.4 1.5 collective-permute-start.5
  32.9 0.5 bitcast_dynamic-update-slice_fusion.17
  33.4 0.5 bitcast_dynamic-update-slice_fusion.16
  33.8 0.5 bitcast_dynamic-update-slice_fusion.15
  34.3 0.5 bitcast_dynamic-update-slice_fusion.14
  34.8 0.5 bitcast_dynamic-update-slice_fusion.13
  35.4 0.5 bitcast_dynamic-update-slice_fusion.12
  35.9 0.5 bitcast_dynamic-update-slice_fusion.11
  36.3 0.5 bitcast_dynamic-update-slice_fusion.10
  36.8 0.5 bitcast_dynamic-update-slice_fusion.9
  37.3 8.8 %fusion.12 = f32[640,1,64]{0,2,1:T(8,128)S(1)} fusion(f32[5760,640]{1,0:T(8,128)S(1)} %bitcast.262, f32[5760,2,64]{0,2,1:T(8,128)S(1)} %copy-done.6), kind=kOutput, calls=%fused_computation.38 | convolution fusion | flops 2831155200 | bytes 16384000 | tf_op jit(solution)/shard_map/dot_general | solution.py:27
  46.3 1.3 collective-permute-start.6
  47.6 4.8 collective-permute-start.7
  52.5 1.5 collective-permute-done.7
  54.6 0.5 bitcast_dynamic-update-slice_fusion.8
  55.0 0.5 bitcast_dynamic-update-slice_fusion.7
  56.4 0.5 bitcast_dynamic-update-slice_fusion.4
  58.8 9.2 %fusion.9 = f32[640,1,64]{0,2,1:T(8,128)S(1)} fusion(f32[5760,640]{1,0:T(8,128)S(1)} %bitcast.264, f32[5760,2,64]{0,2,1:T(8,128)S(1)} %copy-done.6), kind=kOutput, calls=%fused_computation.37 | convolution fusion | flops 2831155200 | bytes 16384000 | tf_op jit(solution)/shard_map/dot_general | solution.py:27
  68.0 2.3 all-gather
  70.7 1.6 reduce_sum.27
  72.3 31.4 %all-gather.6.cloned.1.call-done = f32[2560,2,64]{0,2,1:T(8,128)} async-done(((f32[640,2,64]{0,2,1:T(8,128)}), f32[2560,2,64]{0,2,1:T(8,128)}) %all-gather.6.cloned.1.call-update) | async-done | bytes 1310736 | tf_op jit(solution)/shard_map/all_gather | solution.py:133
  103.7 1.7 reshape.112
  105.5 1.5 reduce_sum.28
  107.1 108.6 %all-gather.8.cloned.1.call-done = f32[20480,2,64]{0,2,1:T(8,128)} async-done(((f32[640,2,64]{0,2,1:T(8,128)}), f32[20480,2,64]{0,2,1:T(8,128)}) %all-gather.8.cloned.1.call-update) | async-done | bytes 10485776 | tf_op jit(solution)/shard_map/all_gather | solution.py:133
  215.8 9.6 %copy.20 = f32[16,8,32,640]{3,2,1,0:T(8,128)} copy(f32[16,8,32,640]{3,1,2,0:T(8,128)} %bitcast.275) | data formatting | bytes 20971520
  225.4 5.6 %reduce_sum.29 = f32[640,2,64]{0,2,1:T(8,128)S(1)} reduce(f32[32,640,2,64]{1,0,3,2:T(8,128)} %bitcast.266, f32[]{:T(128)} %constant.41.clone.1), dimensions={0}, to_apply=%region_2.3 | reduce | flops 2539520 | bytes 10813444 | tf_op jit(solution)/shard_map/reduce_sum | solution.py:133
  231.0 0.5 fusion.62
  231.7 5.8 %cholesky.44 = f32[64,64]{1,0:T(8,128)S(1)} custom-call(f32[64,64]{1,0:T(8,128)S(1)} %get-tuple-element.37), custom_call_target="Cholesky" | custom-call | tf_op jit(solution)/shard_map/jit(cholesky)/cholesky | solution.py:79
  237.5 0.6 compare_reduce_fusion.1
  238.2 0.7 fusion.50
  238.8 4.9 custom-call.6
  244.1 17.1 %convolution_bitcast_fusion.1 = f32[5760,1,64]{0,2,1:T(8,128)S(1)} fusion(f32[5760,640]{1,0:T(8,128)} %bitcast.265, f32[64,640]{1,0:T(8,128)S(1)} %fusion.46), kind=kOutput, calls=%fused_computation.1 | convolution fusion | flops 2831155200 | bytes 16384000 | tf_op jit(solution)/shard_map/dot_general | solution.py:54
  261.3 5.8 %cholesky.55 = f32[64,64]{1,0:T(8,128)S(1)} custom-call(f32[64,64]{1,0:T(8,128)S(1)} %get-tuple-element.36), custom_call_target="Cholesky" | custom-call | tf_op jit(solution)/shard_map/jit(cholesky)/cholesky | solution.py:79
  267.1 0.6 compare_reduce_fusion
  267.8 0.7 fusion.51
  268.4 4.9 custom-call.7
  273.7 17.0 %convolution_bitcast_fusion = f32[5760,1,64]{0,2,1:T(8,128)S(1)} fusion(f32[5760,640]{1,0:T(8,128)} %bitcast.263, f32[64,640]{1,0:T(8,128)S(1)} %fusion.45), kind=kOutput, calls=%fused_computation | convolution fusion | flops 2831155200 | bytes 16384000 | tf_op jit(solution)/shard_map/dot_general | solution.py:54
  290.7 1.8 pad_maximum_fusion
  292.7 0.6 dynamic-slice
  293.9 153.3 %all-reduce.9.cloned.1.call-done = f32[5760,2,64]{0,2,1:T(8,128)} async-done(((f32[5760,2,64]{0,2,1:T(8,128)}), f32[5760,2,64]{0,2,1:T(8,128)}) %all-reduce.9.cloned.1.call-update) | async-done | bytes 2949136
  447.2 1.7 constant_dynamic-slice_fusion
  449.0 28.5 %all-reduce.5.cloned.1.call-done = f32[180,2,64]{0,2,1:T(8,128)} async-done(((f32[180,2,64]{0,2,1:T(8,128)}), f32[180,2,64]{0,2,1:T(8,128)}) %all-reduce.5.cloned.1.call-update) | async-done | bytes 92176 | tf_op jit(solution)/shard_map/psum | solution.py:139
  477.6 0.7 copy.16
  478.3 49.0 %all-reduce.7.cloned.1.call-done = f32[180,2,64]{0,2,1:T(8,128)} async-done(((f32[180,2,64]{0,2,1:T(8,128)}), f32[180,2,64]{0,2,1:T(8,128)}) %all-reduce.7.cloned.1.call-update) | async-done | bytes 92176 | tf_op jit(solution)/shard_map/psum | solution.py:139
  527.3 1.6 copy.41
  (60 shorter events, 6.0 us)
Async XLA Ops:
  7.2 47.4 %copy-start = (bf16[1,16,16,640]{3,2,1,0:T(8,128)(2,1)S(1)}, bf16[1,16,16,640]{3,2,1,0:T(8,128)(2,1)}, u32[]{:S(2)}) copy-start(bf16[1,16,16,640]{3,2,1,0:T(8,128)(2,1)} %param.8) | copy-start | bytes 983044
  7.2 96.6 %all-gather.6.cloned.1.call-start = ((), (), s32[]{:S(2)}) async-start(), calls=%async_computation.2 | async-start | bytes 1638400 | tf_op jit(solution)/shard_map/all_gather | solution.py:133
  7.2 17.9 %copy-start.4 = (bf16[3,3,640,640]{3,2,1,0:T(8,128)(2,1)S(1)}, bf16[3,3,640,640]{3,2,1,0:T(8,128)(2,1)}, u32[]{:S(2)}) copy-start(bf16[3,3,640,640]{3,2,1,0:T(8,128)(2,1)} %param.11) | copy-start | bytes 22118404
  8.1 5.7 %collective-permute-start = (bf16[1,16,640]{2,1,0:T(8,128)(2,1)S(1)}, bf16[1,16,640]{2,1,0:T(8,128)(2,1)S(1)}, u32[]{:S(2)}, u32[]{:S(2)}) collective-permute-start(bf16[1,16,640]{2,1,0:T(8,128)(2,1)S(1)} %get-tuple-element.34), channel_id=1, source_target_pairs={{0,4},{1,5},{2,6},{3,7},{8,12},{9,13},{10,14},{11,15},{16,20},{17,... | collective-permute-start | bytes 61448 | tf_op jit(solution)/shard_map/ppermute | solution.py:14
  10.1 3.7 collective-permute-start.1
  14.9 8.6 %collective-permute-start.2 = (bf16[18,1,640]{2,1,0:T(2,128)(2,1)S(1)}, bf16[18,1,640]{2,1,0:T(2,128)(2,1)S(1)}, u32[]{:S(2)}, u32[]{:S(2)}) collective-permute-start(bf16[18,1,640]{2,1,0:T(2,128)(2,1)S(1)} %get-tuple-element.27), channel_id=1, source_target_pairs={{1,0},{2,1},{3,2},{5,4},{6,5},{7,6},{9,8},{10,9},{11,10},{13,12},{... | collective-permute-start | bytes 69128 | tf_op jit(solution)/shard_map/ppermute | solution.py:15
  16.2 7.3 %collective-permute-start.3 = (bf16[18,1,640]{2,1,0:T(2,128)(2,1)S(1)}, bf16[18,1,640]{2,1,0:T(2,128)(2,1)S(1)}, u32[]{:S(2)}, u32[]{:S(2)}) collective-permute-start(bf16[18,1,640]{2,1,0:T(2,128)(2,1)S(1)} %get-tuple-element.26), channel_id=1, source_target_pairs={{0,1},{1,2},{2,3},{4,5},{5,6},{6,7},{8,9},{9,10},{10,11},{12,13},{... | collective-permute-start | bytes 69128 | tf_op jit(solution)/shard_map/ppermute | solution.py:14
  23.5 3.5 copy-start.5
  27.9 6.9 %copy-start.7 = (bf16[1,16,16,640]{3,2,1,0:T(8,128)(2,1)S(1)}, bf16[1,16,16,640]{3,2,1,0:T(8,128)(2,1)}, u32[]{:S(2)}) copy-start(bf16[1,16,16,640]{3,2,1,0:T(8,128)(2,1)} %param.9) | copy-start | bytes 983044
  28.9 17.2 %collective-permute-start.4 = (bf16[1,16,640]{2,1,0:T(8,128)(2,1)S(1)}, bf16[1,16,640]{2,1,0:T(8,128)(2,1)S(1)}, u32[]{:S(2)}, u32[]{:S(2)}) collective-permute-start(bf16[1,16,640]{2,1,0:T(8,128)(2,1)S(1)} %get-tuple-element.30), channel_id=1, source_target_pairs={{0,4},{1,5},{2,6},{3,7},{8,12},{9,13},{10,14},{11,15},{16,20},{17,... | collective-permute-start | bytes 61448 | tf_op jit(solution)/shard_map/ppermute | solution.py:14
  31.4 14.7 %collective-permute-start.5 = (bf16[1,16,640]{2,1,0:T(8,128)(2,1)S(1)}, bf16[1,16,640]{2,1,0:T(8,128)(2,1)S(1)}, u32[]{:S(2)}, u32[]{:S(2)}) collective-permute-start(bf16[1,16,640]{2,1,0:T(8,128)(2,1)S(1)} %get-tuple-element.31), channel_id=1, source_target_pairs={{4,0},{5,1},{6,2},{7,3},{12,8},{13,9},{14,10},{15,11},{20,16},{21,... | collective-permute-start | bytes 61448 | tf_op jit(solution)/shard_map/ppermute | solution.py:15
  35.4 1.9 copy-start.6
  37.3 8.8 %copy-start.2 = (f32[9,640,640]{2,1,0:T(8,128)}, f32[9,640,640]{2,1,0:T(8,128)S(1)}, u32[]{:S(2)}) copy-start(f32[9,640,640]{2,1,0:T(8,128)S(1)} %bitcast_dynamic-update-slice_fusion.9) | copy-start | bytes 44236804
  46.3 6.3 %collective-permute-start.6 = (bf16[18,1,640]{2,1,0:T(2,128)(2,1)S(1)}, bf16[18,1,640]{2,1,0:T(2,128)(2,1)S(1)}, u32[]{:S(2)}, u32[]{:S(2)}) collective-permute-start(bf16[18,1,640]{2,1,0:T(2,128)(2,1)S(1)} %get-tuple-element.23), channel_id=1, source_target_pairs={{1,0},{2,1},{3,2},{5,4},{6,5},{7,6},{9,8},{10,9},{11,10},{13,12},{... | collective-permute-start | bytes 69128 | tf_op jit(solution)/shard_map/ppermute | solution.py:15
  47.6 6.5 %collective-permute-start.7 = (bf16[18,1,640]{2,1,0:T(2,128)(2,1)S(1)}, bf16[18,1,640]{2,1,0:T(2,128)(2,1)S(1)}, u32[]{:S(2)}, u32[]{:S(2)}) collective-permute-start(bf16[18,1,640]{2,1,0:T(2,128)(2,1)S(1)} %get-tuple-element.22), channel_id=1, source_target_pairs={{0,1},{1,2},{2,3},{4,5},{5,6},{6,7},{8,9},{9,10},{10,11},{12,13},{... | collective-permute-start | bytes 69128 | tf_op jit(solution)/shard_map/ppermute | solution.py:14
  58.8 9.2 %copy-start.3 = (f32[9,640,640]{2,1,0:T(8,128)}, f32[9,640,640]{2,1,0:T(8,128)S(1)}, u32[]{:S(2)}) copy-start(f32[9,640,640]{2,1,0:T(8,128)S(1)} %bitcast_dynamic-update-slice_fusion) | copy-start | bytes 44236804
  72.2 143.5 %all-gather.8.cloned.1.call-start = ((), (), s32[]{:S(2)}) async-start(), calls=%async_computation.3 | async-start | bytes 10813440 | tf_op jit(solution)/shard_map/all_gather | solution.py:133
  107.1 340.2 %all-reduce.9.cloned.1.call-start = ((), (), s32[]{:S(2)}) async-start(), calls=%async_computation.4 | async-start | bytes 5898240
  273.7 255.2 %copy-start.1 = (bf16[1,16,16,640]{3,2,1,0:T(8,128)(2,1)S(1)}, bf16[1,16,16,640]{3,2,1,0:T(8,128)(2,1)}, u32[]{:S(2)}) copy-start(bf16[1,16,16,640]{3,2,1,0:T(8,128)(2,1)} %param.8) | copy-start | bytes 983044
  290.7 1.9 copy-start.8
  292.6 184.9 %all-reduce.5.cloned.1.call-start = ((), (), s32[]{:S(2)}) async-start(), calls=%async_computation | async-start | bytes 262144 | tf_op jit(solution)/shard_map/psum | solution.py:139
  448.9 78.4 %all-reduce.7.cloned.1.call-start = ((), (), s32[]{:S(2)}) async-start(), calls=%async_computation.1 | async-start | bytes 262144 | tf_op jit(solution)/shard_map/psum | solution.py:139
Sparse Core Ops, SparseCore 0:
  72.4 31.3 all-gather.5
  107.2 108.5 all-gather.7
  292.7 154.4 all-reduce.8
  450.4 27.0 all-reduce.4
  479.8 47.5 all-reduce.6
